TPU v7x, 32 devices: a whole 2x2x4 slice. The times are simulated.
32 devices in a mesh: ex: 8 (over z, y), par: 4 (over x, core).
Axes of the slice: x: 2, y: 2, z: 4, core: 2. Of those that a mesh axis runs over, the one named last changes fastest.
Arguments:
- gradients: bfloat16 [512, 16384], P('ex', 'par'), may hold values from -6 to 6
- inverse_gram: bfloat16 [16384, 16384], P('par', 'ex'), may hold values from -1 to 3
- hash_words: int32 [4], replicated, may hold values from 1 to 2147483646
Outputs:
- scores: float32 [512, 512], P('par', 'ex')
All inputs are finite; a program needn't handle non-finite values.
Results may differ from a plain program's by a relative error of at most 0.0003.
Values may be sent and summed in bfloat16 or wider, within the bound.
A program may use at most 64 MiB of HBM per device.

v0:
```python
import functools

import jax
import jax.numpy as jnp
from jax import lax
from jax.experimental import pallas as pl
from jax.experimental.pallas import tpu as pltpu
from jax.sharding import PartitionSpec as P

FEATURES = 16384


def shifted(values, amount):
    return lax.shift_right_logical(values, jnp.full(values.shape, amount, jnp.int32))


def hash_kernel(tile, words_ref, start_ref, cols_ref, grads_ref, out_ref):
    step = pl.program_id(0)
    depth = grads_ref.shape[1]
    m0 = words_ref[0] | 1
    m2 = words_ref[2] | 1
    m3 = words_ref[3] | 1
    row_base = (start_ref[0] + step * depth) * FEATURES * m0 + words_ref[1]
    rows = lax.broadcasted_iota(jnp.int32, (depth, tile), 0) * (m0 * FEATURES)
    grads = grads_ref[...]
    for spot in range(out_ref.shape[0]):
        first = spot * tile
        mixed = rows + (cols_ref[:, first:first + tile] * m0 + row_base)
        mixed = (mixed ^ shifted(mixed, 15)) * m2
        mixed = (mixed ^ shifted(mixed, 13)) * m3
        signs = jnp.where(mixed < 0, -1.0, 1.0).astype(jnp.bfloat16)
        part = jnp.dot(grads, signs, preferred_element_type=jnp.float32)

        @pl.when(step == 0)
        def _():
            out_ref[spot] = part

        @pl.when(step > 0)
        def _():
            out_ref[spot] += part


def project(words, start, cols, grads, tile):
    rows, amount = grads.shape
    width = cols.shape[1]
    depth = min(512, amount)
    return pl.pallas_call(
        functools.partial(hash_kernel, tile),
        grid=(amount // depth,),
        in_specs=[
            pl.BlockSpec(memory_space=pltpu.SMEM),
            pl.BlockSpec(memory_space=pltpu.SMEM),
            pl.BlockSpec((1, width), lambda k: (0, 0)),
            pl.BlockSpec((rows, depth), lambda k: (0, k)),
        ],
        out_specs=pl.BlockSpec((width // tile, rows, tile), lambda k: (0, 0, 0)),
        out_shape=jax.ShapeDtypeStruct((width // tile, rows, tile), jnp.float32),
        compiler_params=pltpu.CompilerParams(
            dimension_semantics=("arbitrary",), vmem_limit_bytes=48 << 20
        ),
    )(words, start, cols, grads)


MESH = pl.DeviceIdType.MESH


def gather_kernel(ex_n, own_ref, out_ref, keep_sem, up_sem, down_sem, side_sem, recv_sem):
    e = lax.axis_index("ex")
    line, side = e // 2, e % 2
    last = ex_n // 2 - 1
    above, below, beside = lax.rem(e + 2, ex_n), lax.rem(e + ex_n - 2, ex_n), line * 2 + 1 - side
    barrier = pltpu.get_barrier_semaphore()

    def greet(peer):
        pl.semaphore_signal(barrier, inc=1, device_id={"ex": peer}, device_id_type=MESH)

    greet(beside)
    pl.when(line < last)(lambda: greet(above))
    pl.when(line > 0)(lambda: greet(below))
    inside = (line > 0) & (line < last)
    pl.when(inside)(lambda: pl.semaphore_wait(barrier, 3))
    pl.when(jnp.logical_not(inside))(lambda: pl.semaphore_wait(barrier, 2))

    def copy(src, slot, sems, peer):
        return pltpu.make_async_remote_copy(
            src_ref=src,
            dst_ref=out_ref.at[slot],
            send_sem=sems.at[slot],
            recv_sem=recv_sem.at[slot],
            device_id={"ex": peer},
            device_id_type=MESH,
        )

    keep = pltpu.make_async_copy(own_ref, out_ref.at[e], keep_sem)
    keep.start()
    pl.when(line < last)(lambda: copy(own_ref, e, up_sem, above).start())
    pl.when(line > 0)(lambda: copy(own_ref, e, down_sem, below).start())
    copy(own_ref, e, side_sem, beside).start()
    for far in range(1, last + 1):
        low, high = e - 2 * far, e + 2 * far

        @pl.when(line >= far)
        def _():
            copy(out_ref.at[low], low, up_sem, above).wait_recv()
            pl.when(line < last)(lambda: copy(out_ref.at[low], low, up_sem, above).start())
            copy(out_ref.at[low], low, side_sem, beside).start()

        @pl.when(line + far <= last)
        def _():
            copy(out_ref.at[high], high, down_sem, below).wait_recv()
            pl.when(line > 0)(lambda: copy(out_ref.at[high], high, down_sem, below).start())
            copy(out_ref.at[high], high, side_sem, beside).start()

    for spot in range(last + 1):
        mine, other = 2 * spot + side, 2 * spot + 1 - side
        copy(out_ref.at[other], other, side_sem, beside).wait_recv()
        copy(out_ref.at[mine], mine, side_sem, beside).wait_send()

        @pl.when((line < last) & (line >= spot))
        def _():
            copy(out_ref.at[mine], mine, up_sem, above).wait_send()

        @pl.when((line > 0) & (line <= spot))
        def _():
            copy(out_ref.at[mine], mine, down_sem, below).wait_send()

    keep.wait()


def gather(ex_n, own, collective_id):
    return pl.pallas_call(
        functools.partial(gather_kernel, ex_n),
        in_specs=[pl.BlockSpec(memory_space=pltpu.VMEM)],
        out_specs=pl.BlockSpec(memory_space=pl.ANY),
        out_shape=jax.ShapeDtypeStruct((ex_n,) + own.shape, own.dtype),
        scratch_shapes=[pltpu.SemaphoreType.DMA]
        + [pltpu.SemaphoreType.DMA((ex_n,)) for _ in range(4)],
        compiler_params=pltpu.CompilerParams(
            collective_id=collective_id, has_side_effects=True, vmem_limit_bytes=8 << 20
        ),
    )(own)


def scatter_kernel(ex_n, scale, in_ref, out_ref, landed, send_sem, recv_sem):
    e = lax.axis_index("ex")
    rows = out_ref.shape[0]
    barrier = pltpu.get_barrier_semaphore()
    for far in range(1, ex_n):
        peer = lax.rem(e + far, ex_n)
        pl.semaphore_signal(barrier, inc=1, device_id={"ex": peer}, device_id_type=MESH)
    pl.semaphore_wait(barrier, ex_n - 1)
    copies = []
    for far in range(1, ex_n):
        peer = lax.rem(e + far, ex_n)
        copies.append(
            pltpu.make_async_remote_copy(
                src_ref=in_ref.at[pl.ds(pl.multiple_of(peer * rows, rows), rows)],
                dst_ref=landed.at[far],
                send_sem=send_sem.at[far],
                recv_sem=recv_sem.at[far],
                device_id={"ex": peer},
                device_id_type=MESH,
            )
        )
        copies[-1].start()
    total = in_ref[pl.ds(pl.multiple_of(e * rows, rows), rows), :]
    for far in range(1, ex_n):
        copies[far - 1].wait_recv()
        total += landed[far]
    out_ref[...] = total * scale
    for each in copies:
        each.wait_send()


def scatter(ex_n, scale, stacked, collective_id):
    rows, columns = stacked.shape[0] // ex_n, stacked.shape[1]
    return pl.pallas_call(
        functools.partial(scatter_kernel, ex_n, scale),
        in_specs=[pl.BlockSpec(memory_space=pltpu.VMEM)],
        out_specs=pl.BlockSpec(memory_space=pltpu.VMEM),
        out_shape=jax.ShapeDtypeStruct((rows, columns), jnp.float32),
        scratch_shapes=[
            pltpu.VMEM((ex_n, rows, columns), jnp.float32),
            pltpu.SemaphoreType.DMA((ex_n,)),
            pltpu.SemaphoreType.DMA((ex_n,)),
        ],
        compiler_params=pltpu.CompilerParams(
            collective_id=collective_id, has_side_effects=True, vmem_limit_bytes=16 << 20
        ),
    )(stacked)


def fold_kernel(chips, cuts, scale, in_ref, out_ref, near, staged, landed, near_send, near_recv, far_send, far_recv):
    p = lax.axis_index("par")
    x, core = p // 2, p % 2
    rows = in_ref.shape[1] // cuts
    partner = x * 2 + 1 - core
    barrier = pltpu.get_barrier_semaphore()
    pl.semaphore_signal(barrier, inc=1, device_id={"par": partner}, device_id_type=MESH)
    for d in range(1, chips):
        peer = lax.rem(x + d, chips) * 2 + core
        pl.semaphore_signal(barrier, inc=1, device_id={"par": peer}, device_id_type=MESH)
    pl.semaphore_wait(barrier, chips)
    order = [(d, c) for d in list(range(1, chips)) + [0] for c in range(cuts)]
    across, onward = {}, {}
    for d, c in order:
        part = pl.ds(c * rows, rows)
        across[d, c] = pltpu.make_async_remote_copy(
            src_ref=in_ref.at[lax.rem(x + d, chips) * 2 + 1 - core, part],
            dst_ref=near.at[d, part],
            send_sem=near_send.at[d, c],
            recv_sem=near_recv.at[d, c],
            device_id={"par": partner},
            device_id_type=MESH,
        )
        across[d, c].start()
    for d, c in order:
        part = pl.ds(c * rows, rows)
        across[d, c].wait_recv()
        total = in_ref[lax.rem(x + d, chips) * 2 + core, part, :] + near[d, part, :]
        staged[d, part, :] = total
        if d > 0:
            onward[d, c] = pltpu.make_async_remote_copy(
                src_ref=staged.at[d, part],
                dst_ref=landed.at[d, part],
                send_sem=far_send.at[d, c],
                recv_sem=far_recv.at[d, c],
                device_id={"par": lax.rem(x + d, chips) * 2 + core},
                device_id_type=MESH,
            )
            onward[d, c].start()
    for c in range(cuts):
        part = pl.ds(c * rows, rows)
        total = staged[0, part, :]
        for d in range(1, chips):
            onward[d, c].wait_recv()
            total += landed[d, part, :]
        out_ref[part, :] = (total * scale).astype(out_ref.dtype)
    for each in list(across.values()) + list(onward.values()):
        each.wait_send()


def fold(scale, stacked, dtype, collective_id):
    par_n, rows, columns = stacked.shape
    chips = par_n // 2
    cuts = 8 if rows * columns >= 1 << 18 else 2
    hold = pltpu.VMEM((chips, rows, columns), jnp.float32)
    return pl.pallas_call(
        functools.partial(fold_kernel, chips, cuts, scale),
        in_specs=[pl.BlockSpec(memory_space=pltpu.VMEM)],
        out_specs=pl.BlockSpec(memory_space=pltpu.VMEM),
        out_shape=jax.ShapeDtypeStruct((rows, columns), dtype),
        scratch_shapes=[hold, hold, hold]
        + [pltpu.SemaphoreType.DMA((chips, cuts)) for _ in range(4)],
        compiler_params=pltpu.CompilerParams(
            collective_id=collective_id, has_side_effects=True, vmem_limit_bytes=48 << 20
        ),
    )(stacked)


def tiles_kernel(feat_ref, gram_ref, out_ref):
    step = pl.program_id(0)
    tile = out_ref.shape[2]
    for spot in range(out_ref.shape[0]):
        gram = gram_ref[:, spot * tile:(spot + 1) * tile]
        part = jnp.dot(feat_ref[0], gram, preferred_element_type=jnp.float32)

        @pl.when(step == 0)
        def _():
            out_ref[spot] = part

        @pl.when(step > 0)
        def _():
            out_ref[spot] += part


def precondition(blocks, gram, tile):
    count, rows, piece = blocks.shape
    width = gram.shape[1]
    return pl.pallas_call(
        tiles_kernel,
        grid=(count,),
        in_specs=[
            pl.BlockSpec((1, rows, piece), lambda k: (k, 0, 0)),
            pl.BlockSpec((piece, width), lambda k: (k, 0)),
        ],
        out_specs=pl.BlockSpec((width // tile, rows, tile), lambda k: (0, 0, 0)),
        out_shape=jax.ShapeDtypeStruct((width // tile, rows, tile), jnp.float32),
        compiler_params=pltpu.CompilerParams(
            dimension_semantics=("arbitrary",), vmem_limit_bytes=48 << 20
        ),
        cost_estimate=pl.CostEstimate(
            flops=2 * count * rows * piece * width,
            bytes_accessed=2 * count * piece * (rows + width) + 4 * rows * width,
            transcendentals=0,
        ),
    )(blocks, gram)


def per_device(ex_n, par_n, gradients, inverse_gram, hash_words):
    amount = gradients.shape[1]
    feat_par, feat_ex = inverse_gram.shape
    piece = feat_par // ex_n
    e, p = lax.axis_index("ex"), lax.axis_index("par")
    ids = jnp.arange(feat_ex, dtype=jnp.int32)
    cols = (ids // piece) * feat_par + e * piece + ids % piece
    everyone = gather(ex_n, gradients, 1).reshape(-1, amount)
    partial = project(hash_words, (p * amount)[None], cols[None, :], everyone, piece)
    mine = fold(FEATURES ** (-0.5), partial, jnp.bfloat16, 4)
    blocks = gather(ex_n, mine, 2)
    mine, blocks = lax.optimization_barrier((mine, blocks))
    pairs = []
    for src_e in range(ex_n):
        for src_p in range(par_n):
            pairs.append((src_e * par_n + src_p, src_p * ex_n + src_e))
    moved = lax.ppermute(mine, ("ex", "par"), pairs)
    parts = precondition(blocks, inverse_gram, piece)
    conditioned = fold(1.0, parts, jnp.bfloat16, 5)
    pairs = lax.dot_general(
        conditioned,
        moved,
        (((1,), (1,)), ((), ())),
        preferred_element_type=jnp.float32,
    )
    rows = fold(1.0, pairs.reshape(par_n, -1, pairs.shape[1]), jnp.float32, 6)
    return scatter(ex_n, FEATURES ** (-0.5), rows.T, 3).T


def solution(mesh):
    return jax.shard_map(
        functools.partial(per_device, mesh.shape["ex"], mesh.shape["par"]),
        mesh=mesh,
        in_specs=(P("ex", "par"), P("par", "ex"), P()),
        out_specs=P("par", "ex"),
        check_vma=False,
    )
```

profile of v0, /device:TPU:0, one launch (start us, length us, event | category | flops | bytes accessed | tf_op | source)
XLA Modules:
  0.0 227.5 jit_solution(9765212060104999458)
XLA Ops:
  0.0 0.0 copy-start.3
  0.0 0.0 copy-start.2
  0.0 1.0 copy-done.2
  1.1 52.5 %shard_map.37 = bf16[8,64,4096]{2,1,0:T(8,128)(2,1)S(1)} custom-call(bf16[64,4096]{1,0:T(8,128)(2,1)S(1)} %copy-done.2), custom_call_target="tpu_custom_call" | custom-call | tf_op jit(solution)/shard_map/pallas_call | solution.py:131
  53.6 0.0 copy-start
  53.6 1.9 copy-done
  55.5 0.0 copy-done.3
  55.5 23.9 %shard_map.38.in_ref = f32[4,512,512]{2,1,0:T(8,128)S(1)} custom-call(s32[4]{0:T(128)S(1)} %copy-done.3, s32[1]{0:T(128)} %bitcast.start_ref, s32[1,2048]{1,0:T(1,128)S(1)} %fusion.cols_ref, bf16[512,4096]{1,0:T(8,128)(2,1)} %bitcast.7), custom_call_target="tpu_custom_call" | custom-call | tf_op jit(solution)/shard_map/pallas_call | solution.py:47
  79.4 27.4 %shard_map.39.own_ref = bf16[512,512]{1,0:T(8,128)(2,1)S(1)} custom-call(f32[4,512,512]{2,1,0:T(8,128)S(1)} %shard_map.38.in_ref), custom_call_target="tpu_custom_call" | custom-call | tf_op jit(solution)/shard_map/pallas_call | solution.py:248
  106.8 49.0 %shard_map.40.feat_ref = bf16[8,512,512]{2,1,0:T(8,128)(2,1)S(1)} custom-call(bf16[512,512]{1,0:T(8,128)(2,1)S(1)} %shard_map.39.own_ref), custom_call_target="tpu_custom_call" | custom-call | tf_op jit(solution)/shard_map/pallas_call | solution.py:131
  155.8 0.0 copy-start.1
  155.8 1.9 copy-done.1
  157.8 0.7 collective-permute-start
  158.5 18.8 %shard_map.41.in_ref = f32[4,512,512]{2,1,0:T(8,128)S(1)} custom-call(bf16[8,512,512]{2,1,0:T(8,128)(2,1)} %copy-done.1, bf16[4096,2048]{1,0:T(8,128)(2,1)} %gram_ref.1), custom_call_target="tpu_custom_call" | custom-call | flops 8589934592 | bytes 25165824 | tf_op jit(solution)/shard_map/pallas_call | solution.py:280
  177.3 29.8 %shard_map.42 = bf16[512,512]{1,0:T(8,128)(2,1)S(1)} custom-call(f32[4,512,512]{2,1,0:T(8,128)S(1)} %shard_map.41.in_ref), custom_call_target="tpu_custom_call" | custom-call | tf_op jit(solution)/shard_map/pallas_call | solution.py:248
  207.1 0.0 collective-permute-done
  207.1 0.5 fusion.3
  207.5 9.7 %shard_map.43 = f32[128,512]{1,0:T(8,128)S(1)} custom-call(f32[4,128,512]{2,1,0:T(8,128)S(1)} %bitcast.8), custom_call_target="tpu_custom_call" | custom-call | tf_op jit(solution)/shard_map/pallas_call | solution.py:248
  217.2 0.1 copy.4
  217.4 9.5 %shard_map.44 = f32[64,128]{1,0:T(8,128)S(1)} custom-call(f32[512,128]{1,0:T(8,128)S(1)} %bitcast.9), custom_call_target="tpu_custom_call" | custom-call | tf_op jit(solution)/shard_map/pallas_call | solution.py:177
  226.8 0.6 copy.6
  (1 shorter events, 0.0 us)
Async XLA Ops:
  0.0 55.5 %copy-start.3 = (s32[4]{0:T(128)S(1)}, s32[4]{0:T(128)}, u32[]{:S(2)}) copy-start(s32[4]{0:T(128)} %words_ref.1) | copy-start | bytes 52
  0.0 1.0 copy-start.2
  53.6 1.9 copy-start
  155.8 1.9 copy-start.1
  157.8 49.3 %collective-permute-start = (bf16[512,512]{1,0:T(8,128)(2,1)S(1)}, bf16[512,512]{1,0:T(8,128)(2,1)S(1)}, u32[]{:S(2)}, u32[]{:S(2)}) collective-permute-start(bf16[512,512]{1,0:T(8,128)(2,1)S(1)} %shard_map.39.own_ref), channel_id=1, source_target_pairs={{0,0},{1,8},{2,16},{3,24},{4,1},{5,9},{6,17},{7,25},{8,2},{9,10},{... | collective-permute-start | bytes 1572872 | tf_op jit(solution)/shard_map/ppermute | solution.py:316
where the time goes:
time: 228 us; the launch traced here: 227 us
  Pallas kernels  221 us (97%)
  local copies, waits for them, and re-layouts  5.64 us (2%)
    pallas_call x2, Pallas kernels, gather(): pl.pallas_call(functools.partial(gather_kernel, ex_n), in_specs=[pl.Block...  101 us
    pallas_call x3, Pallas kernels, fold(): pl.pallas_call(functools.partial(fold_kernel, chips, cuts, scale), in_spe...  66.8 us
    pallas_call x1, Pallas kernels, project(): pl.pallas_call(functools.partial(hash_kernel, tile), grid=(amount // dept...  23.9 us
    pallas_call x1, Pallas kernels, precondition(): pl.pallas_call(tiles_kernel, grid=(count,), in_specs=[pl.BlockSpec((1, ro...  18.8 us
    pallas_call x1, Pallas kernels, scatter(): pl.pallas_call(functools.partial(scatter_kernel, ex_n, scale), in_specs=[...  9.47 us
    unnamed x9, local copies, waits for them, and re-layouts  5.52 us
  transfers between devices with their start and end apart: 1, of which 0 were waited for; matrix products, arithmetic and copies ran while one was open for 0% of the time, Pallas kernels for 21%

commit v1 on v0

--- a/solution.py
+++ b/solution.py
@@ -297,7 +297,431 @@
     )(blocks, gram)
 
 
+def rider(src, dst, send_sem, recv_sem, device_id):
+    return pltpu.make_async_remote_copy(
+        src_ref=src, dst_ref=dst, send_sem=send_sem, recv_sem=recv_sem,
+        device_id=device_id, device_id_type=MESH,
+    )
+
+
+ORDER = ((1, 1), (1, 0), (0, 1), (0, 0))
+
+
+def whole_kernel(
+    ex_n, features, tile, early, depth, words_ref, grads_ref, gram_ref, out_ref,
+    g2, signs, acc, psend, pown, precv, feats, gram, total, near, staged, far, mine,
+    d1_send, d1_recv, d2_send, d2_recv, summed, landed,
+    gram_sem, keep_sem, gy_send, gz_send, gc_send, g_recv, gp_recv, px_send, px_recv,
+    up_sem, down_sem, side_sem, f_recv, fe_send, fe_recv, fe_keep,
+    cc_send, cc_recv, cx_send, cx_recv, d1_ssem, d1_rsem, d2_ssem, d2_rsem, s_send, s_recv,
+):
+    e, p = lax.axis_index("ex"), lax.axis_index("par")
+    z, y, x, c, h, m = e // 2, e % 2, p // 2, p % 2, e // 4, e % 4
+    lines, groups = ex_n // 2, ex_n // 4
+    last = lines - 1
+    half = g2.shape[3]
+    amount = g2.shape[4]
+    count = feats.shape[0]
+    group_rows = feats.shape[3]
+    block = gram.shape[0]
+    piece = block // 4
+    everyone, width = total.shape[1], total.shape[2]
+    scale = features ** -0.5
+
+    def others(own, n):
+        return [lax.rem(own + d, n) for d in range(1, n)]
+
+    barrier = pltpu.get_barrier_semaphore()
+    for peer in others(e, ex_n):
+        pl.semaphore_signal(barrier, inc=1, device_id={"ex": peer}, device_id_type=MESH)
+    for peer in others(p, 4):
+        pl.semaphore_signal(barrier, inc=1, device_id={"par": peer}, device_id_type=MESH)
+    pl.semaphore_wait(barrier, ex_n + 2)
+
+    to_y, to_z = {"ex": e + 1 - 2 * y}, {"ex": e + 2 - 4 * (z % 2)}
+    to_core, to_x = {"par": x * 2 + 1 - c}, {"par": (1 - x) * 2 + c}
+    to_up, to_down = {"ex": lax.rem(e + 2, ex_n)}, {"ex": lax.rem(e + ex_n - 2, ex_n)}
+    my, mz, md = m + 1 - 2 * (m % 2), m + 2 - 4 * (m // 2), 3 - m
+
+    gsends = []
+
+    def gcopy(src, slot, part, sems, k, recv, target):
+        copy = rider(src, g2.at[c, slot, part], sems.at[k], recv.at[slot, part], target)
+        copy.start()
+        gsends.append(copy)
+
+    own = [grads_ref.at[pl.ds(part * half, half)] for part in (0, 1)]
+    keeps = [pltpu.make_async_copy(own[part], g2.at[c, m, part], keep_sem.at[part]) for part in (0, 1)]
+    gcopy(own[0], m, 0, gy_send, 0, g_recv, to_y)
+    gcopy(own[1], m, 1, gz_send, 0, g_recv, to_z)
+    gcopy(own[1], m, 1, gy_send, 1, g_recv, to_y)
+    gcopy(own[0], m, 0, gz_send, 1, g_recv, to_z)
+    for part in (0, 1):
+        keeps[part].start()
+        gcopy(own[part], m, part, gc_send, part, gp_recv, to_core)
+    loads = []
+    for k in range(4):
+        rows = pl.ds(k * piece, piece)
+        loads.append(pltpu.make_async_copy(gram_ref.at[rows], gram.at[rows], gram_sem.at[k]))
+        loads[-1].start()
+
+    def arrived(slot, part, recv, core):
+        spot = g2.at[core, slot, part]
+        rider(spot, spot, gy_send.at[0], recv.at[slot, part], to_y).wait_recv()
+
+    def first_halves():
+        arrived(my, 0, g_recv, c)
+        gcopy(g2.at[c, my, 0], my, 0, gz_send, 2, g_recv, to_z)
+        gcopy(g2.at[c, my, 0], my, 0, gc_send, 2, gp_recv, to_core)
+        arrived(mz, 1, g_recv, c)
+        gcopy(g2.at[c, mz, 1], mz, 1, gy_send, 2, g_recv, to_y)
+        gcopy(g2.at[c, mz, 1], mz, 1, gc_send, 3, gp_recv, to_core)
+
+    def second_halves():
+        arrived(my, 1, g_recv, c)
+        gcopy(g2.at[c, my, 1], my, 1, gc_send, 4, gp_recv, to_core)
+        arrived(mz, 0, g_recv, c)
+        gcopy(g2.at[c, mz, 0], mz, 0, gc_send, 5, gp_recv, to_core)
+
+    def last_halves():
+        for part in (0, 1):
+            arrived(md, part, g_recv, c)
+            gcopy(g2.at[c, md, part], md, part, gc_send, 6 + part, gp_recv, to_core)
+        for slot in range(4):
+            for part in (0, 1):
+                arrived(slot, part, gp_recv, 1 - c)
+        for keep in keeps:
+            keep.wait()
+
+    m0 = words_ref[0] | 1
+    m2 = words_ref[2] | 1
+    m3 = words_ref[3] | 1
+    spots = lax.broadcasted_iota(jnp.int32, (2 * tile, 1), 0)
+    jump = jnp.where(spots < tile, ((1 - x) * 2 + c) * block, (x * 2 + c) * block - tile)
+    offsets = (spots + jump) * m0
+    across = lax.broadcasted_iota(jnp.int32, (1, depth), 1) * (m0 * features)
+    steps = amount // depth
+
+    def make_signs(t, core, step):
+        first = ((x * 2 + core) * amount + step * depth) * features
+        base = (first + m * piece + t * tile) * m0 + words_ref[1]
+        mixed = offsets + (across + base)
+        mixed = (mixed ^ shifted(mixed, 15)) * m2
+        mixed = (mixed ^ shifted(mixed, 13)) * m3
+        return jnp.where(mixed < 0, -1.0, 1.0).astype(jnp.bfloat16)
+
+    def columns(step):
+        return pl.ds(pl.multiple_of(step * depth, depth), depth)
+
+    def add_in(s, core, step):
+        g = g2[core, :, :, :, columns(step)].reshape(group_rows, depth)
+        acc[...] += lax.dot_general(
+            s, g, (((1,), (1,)), ((), ())), preferred_element_type=jnp.float32
+        )
+
+    def prepare(t):
+        @pl.loop(0, 2 * steps)
+        def _(k):
+            signs[t, k] = make_signs(t, k // steps, k % steps)
+
+    prepare(0)
+    if early > 1:
+        prepare(1)
+    first_halves()
+    if early > 2:
+        prepare(2)
+    if early > 3:
+        prepare(3)
+    second_halves()
+    last_halves()
+
+    def slot(t, s):
+        return feats.at[t, s % 4, s // 4]
+
+    def send(t, s, sems, target):
+        return rider(slot(t, s), slot(t, s), sems.at[t, s], f_recv.at[t, s], target)
+
+    def x_copy(t):
+        return rider(psend.at[t], precv.at[t], px_send.at[t], px_recv.at[t], to_x)
+
+    def finish(t):
+        x_copy(t).wait_recv()
+        done = (pown[t] + precv[t]) * scale
+        feats[t, m, h] = done.T.astype(jnp.bfloat16)
+        pl.when(z < last)(lambda: send(t, e, up_sem, to_up).start())
+        pl.when(z > 0)(lambda: send(t, e, down_sem, to_down).start())
+        send(t, e, side_sem, to_y).start()
+
+    def relay(t, hop):
+        @pl.when(z >= hop)
+        def _():
+            low = e - 2 * hop
+            send(t, low, up_sem, to_up).wait_recv()
+            pl.when(z < last)(lambda: send(t, low, up_sem, to_up).start())
+            send(t, low, side_sem, to_y).start()
+
+        @pl.when(z + hop <= last)
+        def _():
+            high = e + 2 * hop
+            send(t, high, down_sem, to_down).wait_recv()
+            pl.when(z > 0)(lambda: send(t, high, down_sem, to_down).start())
+            send(t, high, side_sem, to_y).start()
+
+    def produced(t):
+        psend[t] = acc[:tile]
+        pown[t] = acc[tile:]
+        x_copy(t).start()
+
+    def service(t):
+        pl.when(t >= 1)(lambda: finish(t - 1))
+        for hop in range(1, lines):
+            pl.when(t >= hop + 1)(lambda: relay(t - hop - 1, hop))
+
+    @pl.loop(0, early)
+    def _(t):
+        acc[...] = jnp.zeros_like(acc)
+
+        @pl.loop(0, 2 * steps)
+        def _(k):
+            add_in(signs[t, k], k // steps, k % steps)
+
+        produced(t)
+        service(t)
+
+    @pl.loop(early, count)
+    def _(t):
+        acc[...] = jnp.zeros_like(acc)
+
+        @pl.loop(0, 2 * steps)
+        def _(k):
+            add_in(make_signs(t, k // steps, k % steps), k // steps, k % steps)
+
+        produced(t)
+        service(t)
+
+    for load in loads:
+        load.wait()
+    holder = e // (ex_n // 4)
+    per = width // tile
+
+    def deal(t, q, act):
+        spot = (e % 2) * 2 + q // 2
+        src = feats.at[t, spot]
+        dst = mine.at[t % per]
+
+        @pl.when((p == holder) & (p == q))
+        def _():
+            act(pltpu.make_async_copy(src, dst, fe_keep.at[t % per]), False)
+
+        @pl.when((p == holder) & (p != q))
+        def _():
+            act(rider(src, dst, fe_send.at[t, q // 2], fe_recv.at[t % per], {"par": q}), True)
+
+    def go(copy, remote):
+        copy.start()
+
+    def sent(copy, remote):
+        if remote:
+            copy.wait_send()
+
+    def multiply(t):
+        for line in range(lines):
+            send(t, 2 * line + 1 - y, side_sem, to_y).wait_recv()
+        for q in (t // per, 2 + t // per):
+            deal(t, q, go)
+        lhs = jnp.concatenate([feats[t, k].reshape(everyone, tile) for k in range(4)], axis=1)
+        for q in range(4):
+            cols = pl.ds(q * width, width)
+            rhs = jnp.concatenate(
+                [gram[k * piece + t * tile:k * piece + (t + 1) * tile, q * width:(q + 1) * width] for k in range(4)], axis=0
+            )
+            part = jnp.dot(lhs, rhs, preferred_element_type=jnp.float32)
+            if t == 0:
+                total[q] = part
+            else:
+                total[q] += part
+
+    events = []
+    finish(count - 1)
+    ready = 0
+    for t in range(count, count + lines - 1):
+        for hop in range(1, lines):
+            if t - hop - 1 < count:
+                relay(t - hop - 1, hop)
+            if hop % 2 == 1 and ready < count - 2:
+                multiply(ready)
+                ready += 1
+    relay(count - 1, last) if lines > 1 else None
+    for t in range(ready, count):
+        multiply(t)
+
+    rows_of = everyone // 4
+
+    def rows(owner):
+        return pl.ds(pl.multiple_of(owner * rows_of, rows_of), rows_of)
+
+    def place(dx, dc, sx, sc):
+        return ((sx + dx) % 2) * 2 + (sc + dc) % 2
+
+    def near_copy(qx, owner):
+        return rider(
+            total.at[qx * 2 + 1 - c, rows(owner)], near.at[qx, rows(owner)],
+            cc_send.at[qx, owner], cc_recv.at[qx, owner], to_core,
+        )
+
+    def far_copy(owner):
+        return rider(
+            staged.at[rows(owner)], far.at[rows(owner)], cx_send.at[owner], cx_recv.at[owner], to_x
+        )
+
+    for dx, dc in ORDER:
+        near_copy(1 - x, place(dx, dc, 1 - x, 1 - c)).start()
+    for dx, dc in ORDER:
+        near_copy(x, place(dx, dc, x, 1 - c)).start()
+    for dx, dc in ORDER:
+        owner = place(dx, dc, 1 - x, c)
+        near_copy(1 - x, owner).wait_recv()
+        staged[rows(owner), :] = total[(1 - x) * 2 + c, rows(owner), :] + near[1 - x, rows(owner), :]
+        far_copy(owner).start()
+
+    for k in range(per):
+        q_spot = mine.at[k]
+
+        @pl.when(p == holder)
+        def _():
+            pltpu.make_async_copy(q_spot, q_spot, fe_keep.at[k]).wait()
+
+        @pl.when(p != holder)
+        def _():
+            rider(q_spot, q_spot, fe_send.at[0, 0], fe_recv.at[k], to_core).wait_recv()
+
+    def d1_copy(k):
+        return rider(d1_send.at[k], d1_recv.at[k], d1_ssem.at[k], d1_rsem.at[k], to_core)
+
+    d2_copy = rider(d2_send, d2_recv, d2_ssem, d2_rsem, to_x)
+    for dx, dc in ORDER:
+        owner = place(dx, dc, x, c)
+        near_copy(x, owner).wait_recv()
+        half_sum = total[x * 2 + c, rows(owner), :] + near[x, rows(owner), :]
+        far_copy(owner).wait_recv()
+        done = (half_sum + far[rows(owner), :]).astype(jnp.bfloat16)
+        rhs = jnp.concatenate([mine[k].reshape(everyone, tile) for k in range(per)], axis=1)
+        part = lax.dot_general(
+            rhs, done, (((1,), (1,)), ((), ())), preferred_element_type=jnp.float32
+        )
+        if dc == 1:
+            d1_send[1 - dx] = part
+            d1_copy(1 - dx).start()
+        elif dx == 1:
+            d1_copy(0).wait_recv()
+            d2_send[...] = part + d1_recv[0]
+            d2_copy.start()
+        else:
+            d1_copy(1).wait_recv()
+            part = part + d1_recv[1]
+            d2_copy.wait_recv()
+            part = part + d2_recv[...]
+            summed[...] = part.reshape(summed.shape)
+
+    def last_copy(k):
+        peer = lax.rem(e + k, ex_n)
+        return rider(summed.at[peer], landed.at[k], s_send.at[k], s_recv.at[k], {"ex": peer})
+
+    for k in range(1, ex_n):
+        last_copy(k).start()
+    final = summed[e]
+    for k in range(1, ex_n):
+        last_copy(k).wait_recv()
+        final += landed[k]
+    out_ref[...] = (final * scale).T
+
+    for copy in gsends:
+        copy.wait_send()
+    for t in range(count):
+        x_copy(t).wait_send()
+        for q in (t // per, 2 + t // per):
+            deal(t, q, sent)
+        send(t, e, side_sem, to_y).wait_send()
+        for line in range(lines):
+            s = 2 * line + y
+            pl.when(line != z)(lambda: send(t, s, side_sem, to_y).wait_send())
+            pl.when((z < last) & (z >= line))(lambda: send(t, s, up_sem, to_up).wait_send())
+            pl.when((z > 0) & (z <= line))(lambda: send(t, s, down_sem, to_down).wait_send())
+    for owner in range(4):
+        near_copy(0, owner).wait_send()
+        near_copy(1, owner).wait_send()
+        far_copy(owner).wait_send()
+    d1_copy(0).wait_send()
+    d1_copy(1).wait_send()
+    d2_copy.wait_send()
+    for k in range(1, ex_n):
+        last_copy(k).wait_send()
+
+
+def fused(ex_n, par_n, gradients, inverse_gram, hash_words):
+    rows, amount = gradients.shape
+    block, width_e = inverse_gram.shape
+    features, everyone = block * par_n, rows * ex_n
+    tile, depth = 128, min(2048, amount)
+    count, width, groups = block // 4 // tile, width_e // 4, ex_n // 4
+    early = min(4, count)
+    group = 4 * rows
+    owned = everyone // 4
+    vmem, dma, f32, bf16 = pltpu.VMEM, pltpu.SemaphoreType.DMA, jnp.float32, jnp.bfloat16
+    return pl.pallas_call(
+        functools.partial(whole_kernel, ex_n, features, tile, early, depth),
+        in_specs=[
+            pl.BlockSpec(memory_space=pltpu.SMEM),
+            pl.BlockSpec(memory_space=pl.ANY),
+            pl.BlockSpec(memory_space=pl.ANY),
+        ],
+        out_specs=pl.BlockSpec(memory_space=pltpu.VMEM),
+        out_shape=jax.ShapeDtypeStruct((owned, rows), f32),
+        scratch_shapes=[
+            vmem((2, 4, 2, rows // 2, amount), bf16),
+            vmem((early, 2 * amount // depth, 2 * tile, depth), bf16),
+            vmem((2 * tile, group), f32),
+            vmem((count, tile, group), f32),
+            vmem((count, tile, group), f32),
+            vmem((count, tile, group), f32),
+            vmem((count, 4, groups, group, tile), bf16),
+            vmem((block, width_e), bf16),
+            vmem((4, everyone, width), f32),
+            vmem((2, everyone, width), f32),
+            vmem((everyone, width), f32),
+            vmem((everyone, width), f32),
+            vmem((width // tile, groups, group, tile), bf16),
+            vmem((2, everyone, owned), f32),
+            vmem((2, everyone, owned), f32),
+            vmem((everyone, owned), f32),
+            vmem((everyone, owned), f32),
+            vmem((ex_n, rows, owned), f32),
+            vmem((ex_n, rows, owned), f32),
+            dma((4,)), dma((2,)), dma((3,)), dma((3,)), dma((8,)), dma((4, 2)), dma((4, 2)),
+            dma((count,)), dma((count,)),
+            dma((count, ex_n)), dma((count, ex_n)), dma((count, ex_n)), dma((count, ex_n)),
+            dma((count, 2)), dma((width // tile,)), dma((width // tile,)),
+            dma((2, 4)), dma((2, 4)), dma((4,)), dma((4,)),
+            dma((2,)), dma((2,)), dma, dma, dma((ex_n,)), dma((ex_n,)),
+        ],
+        compiler_params=pltpu.CompilerParams(
+            collective_id=7, has_side_effects=True, vmem_limit_bytes=66_000_000
+        ),
+    )(hash_words, gradients, inverse_gram)
+
+
+def fits(ex_n, par_n, gradients, inverse_gram):
+    rows = gradients.shape[0]
+    block, width_e = inverse_gram.shape
+    return (
+        par_n == 4 and ex_n == 2 * par_n and width_e % 512 == 0 and block % 512 == 0
+        and rows % 32 == 0 and rows * ex_n % 512 == 0
+    )
+
+
 def per_device(ex_n, par_n, gradients, inverse_gram, hash_words):
+    if fits(ex_n, par_n, gradients, inverse_gram):
+        return fused(ex_n, par_n, gradients, inverse_gram, hash_words)
     amount = gradients.shape[1]
     feat_par, feat_ex = inverse_gram.shape
     piece = feat_par // ex_n

time: 228 us -> 127 us (0.56)
  Pallas kernels: 221 us -> 125 us
  local copies, waits for them, and re-layouts: 5.64 us -> 1.54 us
    pallas_call x8 -> x1, Pallas kernels: 221 us -> 125 us  [fused(): pl.pallas_call(functools.partial(whole_kernel, ex_n, features, tile, earl...]
    unnamed x9 -> x0, local copies, waits for them, and re-layouts: 5.52 us -> none
  transfers between devices with their start and end apart: 1 -> 0, of which waited for: 0 -> 0; matrix products, arithmetic and copies ran while one was open for 0% -> 0% of each run, Pallas kernels for 21% -> 0%
where the time goes in v1:
time: 127 us
  Pallas kernels  125 us (98%)
  local copies, waits for them, and re-layouts  1.54 us (1%)
    pallas_call x1, Pallas kernels, fused(): pl.pallas_call(functools.partial(whole_kernel, ex_n, features, tile, earl...  125 us

profile of v1, /device:TPU:0, one launch (start us, length us, event | category | flops | bytes accessed | tf_op | source)
XLA Modules:
  0.0 126.6 jit_solution(14636516375595750135)
XLA Ops:
  0.0 125.0 %shard_map.37 = f32[128,64]{1,0:T(8,128)} custom-call(s32[4]{0:T(128)} %words_ref.1, bf16[64,4096]{1,0:T(8,128)(2,1)} %grads_ref.1, bf16[4096,2048]{1,0:T(8,128)(2,1)} %gram_ref.1), custom_call_target="tpu_custom_call" | custom-call | tf_op jit(solution)/shard_map/pallas_call | solution.py:671
  125.1 1.5 %copy.4 = f32[128,64]{0,1:T(8,128)} copy(f32[128,64]{1,0:T(8,128)} %shard_map.37) | data formatting | bytes 65536 | tf_op jit(solution)/shard_map/pallas_call | solution.py:671

commit v2 on v1

--- a/solution.py
+++ b/solution.py
@@ -304,16 +304,13 @@
     )
 
 
-ORDER = ((1, 1), (1, 0), (0, 1), (0, 0))
-
-
 def whole_kernel(
     ex_n, features, tile, early, depth, words_ref, grads_ref, gram_ref, out_ref,
-    g2, signs, acc, psend, pown, precv, feats, gram, total, near, staged, far, mine,
-    d1_send, d1_recv, d2_send, d2_recv, summed, landed,
+    g2, signs, acc, psend, pown, precv, feats, gram, total, near, staged, far, marks, far_marks,
+    mine, pairs, landed,
     gram_sem, keep_sem, gy_send, gz_send, gc_send, g_recv, gp_recv, px_send, px_recv,
     up_sem, down_sem, side_sem, f_recv, fe_send, fe_recv, fe_keep,
-    cc_send, cc_recv, cx_send, cx_recv, d1_ssem, d1_rsem, d2_ssem, d2_rsem, s_send, s_recv,
+    cc_send, cc_recv, cx_send, cx_recv, cm_send, cm_recv, s_send, s_recv,
 ):
     e, p = lax.axis_index("ex"), lax.axis_index("par")
     z, y, x, c, h, m = e // 2, e % 2, p // 2, p % 2, e // 4, e % 4
@@ -501,34 +498,42 @@
 
     for load in loads:
         load.wait()
+    per = width // tile
     holder = e // (ex_n // 4)
-    per = width // tile
-
-    def deal(t, q, act):
-        spot = (e % 2) * 2 + q // 2
-        src = feats.at[t, spot]
-        dst = mine.at[t % per]
-
-        @pl.when((p == holder) & (p == q))
-        def _():
-            act(pltpu.make_async_copy(src, dst, fe_keep.at[t % per]), False)
-
-        @pl.when((p == holder) & (p != q))
-        def _():
-            act(rider(src, dst, fe_send.at[t, q // 2], fe_recv.at[t % per], {"par": q}), True)
-
-    def go(copy, remote):
-        copy.start()
-
-    def sent(copy, remote):
-        if remote:
-            copy.wait_send()
+    keeper = p == holder
+    across_x = (x != holder // 2) & (c == holder % 2)
+    behind = (x != holder // 2) & (c != holder % 2)
+
+    def deal(t):
+        return feats.at[t, pl.ds((e % 2) * 2, 2)]
+
+    def deal_keep(t):
+        return pltpu.make_async_copy(deal(t), mine.at[t], fe_keep.at[t])
+
+    def deal_out(t, k):
+        return rider(deal(t), mine.at[t], fe_send.at[t, k], fe_recv.at[t], (to_core, to_x)[k])
+
+    def deal_on(t):
+        return rider(mine.at[t], mine.at[t], fe_send.at[t, 0], fe_recv.at[t], to_core)
+
+    def hand_on(t):
+        @pl.when(across_x)
+        def _():
+            deal_on(t).wait_recv()
+            deal_on(t).start()
 
     def multiply(t):
         for line in range(lines):
             send(t, 2 * line + 1 - y, side_sem, to_y).wait_recv()
-        for q in (t // per, 2 + t // per):
-            deal(t, q, go)
+
+        @pl.when(keeper)
+        def _():
+            deal_keep(t).start()
+            deal_out(t, 1).start()
+            deal_out(t, 0).start()
+
+        if t >= 2:
+            hand_on(t - 2)
         lhs = jnp.concatenate([feats[t, k].reshape(everyone, tile) for k in range(4)], axis=1)
         for q in range(4):
             cols = pl.ds(q * width, width)
@@ -541,7 +546,6 @@
             else:
                 total[q] += part
 
-    events = []
     finish(count - 1)
     ready = 0
     for t in range(count, count + lines - 1):
@@ -555,105 +559,100 @@
     for t in range(ready, count):
         multiply(t)
 
+    for t in range(count - 2, count):
+        hand_on(t)
     rows_of = everyone // 4
-
-    def rows(owner):
-        return pl.ds(pl.multiple_of(owner * rows_of, rows_of), rows_of)
-
-    def place(dx, dc, sx, sc):
-        return ((sx + dx) % 2) * 2 + (sc + dc) % 2
-
-    def near_copy(qx, owner):
+    here = pl.ds(pl.multiple_of(p * rows_of, rows_of), rows_of)
+
+    def rows(qx, qc):
+        return pl.ds(pl.multiple_of((qx * 2 + qc) * rows_of, rows_of), rows_of)
+
+    def near_copy(qx, q):
         return rider(
-            total.at[qx * 2 + 1 - c, rows(owner)], near.at[qx, rows(owner)],
-            cc_send.at[qx, owner], cc_recv.at[qx, owner], to_core,
+            total.at[q, rows(qx, 1 - c)], near.at[qx, q],
+            cc_send.at[qx, q], cc_recv.at[qx, q], to_core,
         )
 
-    def far_copy(owner):
-        return rider(
-            staged.at[rows(owner)], far.at[rows(owner)], cx_send.at[owner], cx_recv.at[owner], to_x
+    def far_copy(q):
+        return rider(staged.at[q], far.at[q], cx_send.at[q], cx_recv.at[q], to_x)
+
+    def mark_copy(q):
+        return rider(marks.at[q], far_marks.at[q], cm_send.at[q], cm_recv.at[q], to_x)
+
+    for qx in (1 - x, x):
+        for q in range(4):
+            near_copy(qx, q).start()
+    for q in range(4):
+        near_copy(1 - x, q).wait_recv()
+        part = total[q, rows(1 - x, c), :] + near[1 - x, q]
+        most = jnp.max(jnp.abs(part), axis=1, keepdims=True)
+        level = jnp.where(most > 0, 32767.0 / most, 0.0)
+        staged[q] = jnp.round(part * level).astype(jnp.int32).astype(jnp.int16)
+        marks[q] = jnp.broadcast_to(most * (1.0 / 32767.0), (rows_of, rows_of)).T[:8]
+        mark_copy(q).start()
+        far_copy(q).start()
+
+    def got_mine(t):
+        pl.when(keeper)(lambda: deal_keep(t).wait())
+        pl.when(jnp.logical_not(keeper | across_x))(lambda: deal_on(t).wait_recv())
+
+    for q in range(4):
+        near_copy(x, q).wait_recv()
+        part = total[q, here, :] + near[x, q]
+        first = (q % 2) * per
+        for t in range(first, first + per):
+            if q < 2:
+                got_mine(t)
+        lhs = jnp.concatenate(
+            [mine[t, q // 2].reshape(everyone, tile) for t in range(first, first + per)], axis=1
         )
-
-    for dx, dc in ORDER:
-        near_copy(1 - x, place(dx, dc, 1 - x, 1 - c)).start()
-    for dx, dc in ORDER:
-        near_copy(x, place(dx, dc, x, 1 - c)).start()
-    for dx, dc in ORDER:
-        owner = place(dx, dc, 1 - x, c)
-        near_copy(1 - x, owner).wait_recv()
-        staged[rows(owner), :] = total[(1 - x) * 2 + c, rows(owner), :] + near[1 - x, rows(owner), :]
-        far_copy(owner).start()
-
-    for k in range(per):
-        q_spot = mine.at[k]
-
-        @pl.when(p == holder)
-        def _():
-            pltpu.make_async_copy(q_spot, q_spot, fe_keep.at[k]).wait()
-
-        @pl.when(p != holder)
-        def _():
-            rider(q_spot, q_spot, fe_send.at[0, 0], fe_recv.at[k], to_core).wait_recv()
-
-    def d1_copy(k):
-        return rider(d1_send.at[k], d1_recv.at[k], d1_ssem.at[k], d1_rsem.at[k], to_core)
-
-    d2_copy = rider(d2_send, d2_recv, d2_ssem, d2_rsem, to_x)
-    for dx, dc in ORDER:
-        owner = place(dx, dc, x, c)
-        near_copy(x, owner).wait_recv()
-        half_sum = total[x * 2 + c, rows(owner), :] + near[x, rows(owner), :]
-        far_copy(owner).wait_recv()
-        done = (half_sum + far[rows(owner), :]).astype(jnp.bfloat16)
-        rhs = jnp.concatenate([mine[k].reshape(everyone, tile) for k in range(per)], axis=1)
-        part = lax.dot_general(
-            rhs, done, (((1,), (1,)), ((), ())), preferred_element_type=jnp.float32
-        )
-        if dc == 1:
-            d1_send[1 - dx] = part
-            d1_copy(1 - dx).start()
-        elif dx == 1:
-            d1_copy(0).wait_recv()
-            d2_send[...] = part + d1_recv[0]
-            d2_copy.start()
+        mark_copy(q).wait_recv()
+        mark = jnp.broadcast_to(far_marks[q][:1], (rows_of, rows_of)).T
+        far_copy(q).wait_recv()
+        other = far[q].astype(jnp.int32).astype(jnp.float32)
+        done = (part + other * jnp.concatenate([mark] * (width // rows_of), axis=1)).astype(jnp.bfloat16)
+        scores = lax.dot_general(
+            lhs, done, (((1,), (1,)), ((), ())), preferred_element_type=jnp.float32
+        ).reshape(pairs.shape)
+        if q == 0:
+            pairs[...] = scores
         else:
-            d1_copy(1).wait_recv()
-            part = part + d1_recv[1]
-            d2_copy.wait_recv()
-            part = part + d2_recv[...]
-            summed[...] = part.reshape(summed.shape)
+            pairs[...] += scores
 
     def last_copy(k):
         peer = lax.rem(e + k, ex_n)
-        return rider(summed.at[peer], landed.at[k], s_send.at[k], s_recv.at[k], {"ex": peer})
+        return rider(pairs.at[peer], landed.at[k], s_send.at[k], s_recv.at[k], {"ex": peer})
 
     for k in range(1, ex_n):
         last_copy(k).start()
-    final = summed[e]
+    final = pairs[e]
     for k in range(1, ex_n):
         last_copy(k).wait_recv()
         final += landed[k]
-    out_ref[...] = (final * scale).T
+    out_ref[...] = final * scale
 
     for copy in gsends:
         copy.wait_send()
     for t in range(count):
         x_copy(t).wait_send()
-        for q in (t // per, 2 + t // per):
-            deal(t, q, sent)
+
+        @pl.when(keeper)
+        def _():
+            deal_out(t, 1).wait_send()
+            deal_out(t, 0).wait_send()
+
+        pl.when(across_x)(lambda: deal_on(t).wait_send())
         send(t, e, side_sem, to_y).wait_send()
         for line in range(lines):
             s = 2 * line + y
             pl.when(line != z)(lambda: send(t, s, side_sem, to_y).wait_send())
             pl.when((z < last) & (z >= line))(lambda: send(t, s, up_sem, to_up).wait_send())
             pl.when((z > 0) & (z <= line))(lambda: send(t, s, down_sem, to_down).wait_send())
-    for owner in range(4):
-        near_copy(0, owner).wait_send()
-        near_copy(1, owner).wait_send()
-        far_copy(owner).wait_send()
-    d1_copy(0).wait_send()
-    d1_copy(1).wait_send()
-    d2_copy.wait_send()
+    for q in range(4):
+        near_copy(0, q).wait_send()
+        near_copy(1, q).wait_send()
+        far_copy(q).wait_send()
+        mark_copy(q).wait_send()
     for k in range(1, ex_n):
         last_copy(k).wait_send()
 
@@ -664,7 +663,7 @@
     features, everyone = block * par_n, rows * ex_n
     tile, depth = 128, min(2048, amount)
     count, width, groups = block // 4 // tile, width_e // 4, ex_n // 4
-    early = min(4, count)
+    early = 4
     group = 4 * rows
     owned = everyone // 4
     vmem, dma, f32, bf16 = pltpu.VMEM, pltpu.SemaphoreType.DMA, jnp.float32, jnp.bfloat16
@@ -676,7 +675,7 @@
             pl.BlockSpec(memory_space=pl.ANY),
         ],
         out_specs=pl.BlockSpec(memory_space=pltpu.VMEM),
-        out_shape=jax.ShapeDtypeStruct((owned, rows), f32),
+        out_shape=jax.ShapeDtypeStruct((rows, owned), f32),
         scratch_shapes=[
             vmem((2, 4, 2, rows // 2, amount), bf16),
             vmem((early, 2 * amount // depth, 2 * tile, depth), bf16),
@@ -687,22 +686,20 @@
             vmem((count, 4, groups, group, tile), bf16),
             vmem((block, width_e), bf16),
             vmem((4, everyone, width), f32),
-            vmem((2, everyone, width), f32),
-            vmem((everyone, width), f32),
-            vmem((everyone, width), f32),
-            vmem((width // tile, groups, group, tile), bf16),
-            vmem((2, everyone, owned), f32),
-            vmem((2, everyone, owned), f32),
-            vmem((everyone, owned), f32),
-            vmem((everyone, owned), f32),
+            vmem((2, 4, owned, width), f32),
+            vmem((4, owned, width), jnp.int16),
+            vmem((4, owned, width), jnp.int16),
+            vmem((4, 8, owned), f32),
+            vmem((4, 8, owned), f32),
+            vmem((count, 2, groups, group, tile), bf16),
             vmem((ex_n, rows, owned), f32),
             vmem((ex_n, rows, owned), f32),
             dma((4,)), dma((2,)), dma((3,)), dma((3,)), dma((8,)), dma((4, 2)), dma((4, 2)),
             dma((count,)), dma((count,)),
             dma((count, ex_n)), dma((count, ex_n)), dma((count, ex_n)), dma((count, ex_n)),
-            dma((count, 2)), dma((width // tile,)), dma((width // tile,)),
-            dma((2, 4)), dma((2, 4)), dma((4,)), dma((4,)),
-            dma((2,)), dma((2,)), dma, dma, dma((ex_n,)), dma((ex_n,)),
+            dma((count, 2)), dma((count,)), dma((count,)),
+            dma((2, 4)), dma((2, 4)), dma((4,)), dma((4,)), dma((4,)), dma((4,)),
+            dma((ex_n,)), dma((ex_n,)),
         ],
         compiler_params=pltpu.CompilerParams(
             collective_id=7, has_side_effects=True, vmem_limit_bytes=66_000_000
@@ -714,14 +711,14 @@
     rows = gradients.shape[0]
     block, width_e = inverse_gram.shape
     return (
-        par_n == 4 and ex_n == 2 * par_n and width_e % 512 == 0 and block % 512 == 0
+        par_n == 4 and ex_n == 2 * par_n and block % 4096 == 0 and width_e % (rows * ex_n) == 0
         and rows % 32 == 0 and rows * ex_n % 512 == 0
     )
 
 
 def per_device(ex_n, par_n, gradients, inverse_gram, hash_words):
     if fits(ex_n, par_n, gradients, inverse_gram):
-        return fused(ex_n, par_n, gradients, inverse_gram, hash_words)
+        return fused(ex_n, par_n, gradients, inverse_gram, hash_words).T
     amount = gradients.shape[1]
     feat_par, feat_ex = inverse_gram.shape
     piece = feat_par // ex_n

time: 127 us -> 115 us (0.906)
  Pallas kernels: 125 us -> 113 us
    pallas_call x1, Pallas kernels: 125 us -> 113 us  [fused(): pl.pallas_call(functools.partial(whole_kernel, ex_n, features, tile, earl...]
    pallas_call x1 -> x0, local copies, waits for them, and re-layouts: 1.54 us -> none  [fused(): pl.pallas_call(functools.partial(whole_kernel, ex_n, features, tile, earl...]
    unnamed x0 -> x1, local copies, waits for them, and re-layouts: none -> 1.38 us
where the time goes in v2:
time: 115 us
  Pallas kernels  113 us (98%)
  local copies, waits for them, and re-layouts  1.38 us (1%)
    pallas_call x1, Pallas kernels, fused(): pl.pallas_call(functools.partial(whole_kernel, ex_n, features, tile, earl...  113 us

profile of v2, /device:TPU:0, one launch (start us, length us, event | category | flops | bytes accessed | tf_op | source)
XLA Modules:
  0.0 114.7 jit_solution(4666018702985712029)
XLA Ops:
  0.0 113.3 %shard_map.37 = f32[64,128]{1,0:T(8,128)} custom-call(s32[4]{0:T(128)} %words_ref.1, bf16[64,4096]{1,0:T(8,128)(2,1)} %grads_ref.1, bf16[4096,2048]{1,0:T(8,128)(2,1)} %gram_ref.1), custom_call_target="tpu_custom_call" | custom-call | tf_op jit(solution)/shard_map/pallas_call | solution.py:670
  113.3 1.4 %copy.5 = f32[128,64]{0,1:T(8,128)} copy(f32[128,64]{0,1:T(8,128)} %bitcast.1) | data formatting | bytes 65536

commit v3 on v2

--- a/solution.py
+++ b/solution.py
@@ -449,20 +449,39 @@
         pl.when(z > 0)(lambda: send(t, e, down_sem, to_down).start())
         send(t, e, side_sem, to_y).start()
 
+    def bends(t):
+        return (t % 2 == 1) & (t < count - 1)
+
+    def crosses(t, line):
+        return jnp.logical_not(bends(t)) | ((line > 0) & (line < last))
+
     def relay(t, hop):
         @pl.when(z >= hop)
         def _():
             low = e - 2 * hop
             send(t, low, up_sem, to_up).wait_recv()
             pl.when(z < last)(lambda: send(t, low, up_sem, to_up).start())
-            send(t, low, side_sem, to_y).start()
+            pl.when(crosses(t, z - hop))(lambda: send(t, low, side_sem, to_y).start())
 
         @pl.when(z + hop <= last)
         def _():
             high = e + 2 * hop
             send(t, high, down_sem, to_down).wait_recv()
             pl.when(z > 0)(lambda: send(t, high, down_sem, to_down).start())
-            send(t, high, side_sem, to_y).start()
+            pl.when(crosses(t, z + hop))(lambda: send(t, high, side_sem, to_y).start())
+
+    first_far, last_far = 1 - y, 2 * last + 1 - y
+
+    def detour(t, hop):
+        @pl.when(bends(t) & (t > 0) & (z == hop - 1))
+        def _():
+            send(t, first_far, up_sem, to_up).wait_recv()
+            pl.when(z < last)(lambda: send(t, first_far, up_sem, to_up).start())
+
+        @pl.when(bends(t) & (t > 0) & (last - z == hop - 1))
+        def _():
+            send(t, last_far, down_sem, to_down).wait_recv()
+            pl.when(z > 0)(lambda: send(t, last_far, down_sem, to_down).start())
 
     def produced(t):
         psend[t] = acc[:tile]
@@ -473,6 +492,8 @@
         pl.when(t >= 1)(lambda: finish(t - 1))
         for hop in range(1, lines):
             pl.when(t >= hop + 1)(lambda: relay(t - hop - 1, hop))
+        for hop in range(1, lines):
+            detour(t - hop - 2, hop)
 
     @pl.loop(0, early)
     def _(t):
@@ -523,14 +544,19 @@
             deal_on(t).start()
 
     def multiply(t):
+        bent = t % 2 == 1 and t < count - 1
+        if bent:
+            detour(t, lines)
         for line in range(lines):
-            send(t, 2 * line + 1 - y, side_sem, to_y).wait_recv()
+            if not bent or 0 < line < last:
+                send(t, 2 * line + 1 - y, side_sem, to_y).wait_recv()
 
         @pl.when(keeper)
         def _():
             deal_keep(t).start()
-            deal_out(t, 1).start()
             deal_out(t, 0).start()
+            if t < count - 1:
+                deal_out(t, 1).start()
 
         if t >= 2:
             hand_on(t - 2)
@@ -548,19 +574,18 @@
 
     finish(count - 1)
     ready = 0
-    for t in range(count, count + lines - 1):
+    for t in range(count, count + lines):
         for hop in range(1, lines):
             if t - hop - 1 < count:
                 relay(t - hop - 1, hop)
-            if hop % 2 == 1 and ready < count - 2:
+            if (t - hop - 2) % 2 == 1 and t - hop - 2 < count - 1:
+                detour(t - hop - 2, hop)
+            if hop % 2 == 1 and ready < count - 4:
                 multiply(ready)
                 ready += 1
-    relay(count - 1, last) if lines > 1 else None
     for t in range(ready, count):
         multiply(t)
 
-    for t in range(count - 2, count):
-        hand_on(t)
     rows_of = everyone // 4
     here = pl.ds(pl.multiple_of(p * rows_of, rows_of), rows_of)
 
@@ -579,10 +604,11 @@
     def mark_copy(q):
         return rider(marks.at[q], far_marks.at[q], cm_send.at[q], cm_recv.at[q], to_x)
 
+    sequence = (0, 2, 1, 3)
     for qx in (1 - x, x):
-        for q in range(4):
+        for q in sequence:
             near_copy(qx, q).start()
-    for q in range(4):
+    for q in sequence:
         near_copy(1 - x, q).wait_recv()
         part = total[q, rows(1 - x, c), :] + near[1 - x, q]
         most = jnp.max(jnp.abs(part), axis=1, keepdims=True)
@@ -591,12 +617,16 @@
         marks[q] = jnp.broadcast_to(most * (1.0 / 32767.0), (rows_of, rows_of)).T[:8]
         mark_copy(q).start()
         far_copy(q).start()
+        if q == sequence[2]:
+            pl.when(keeper)(lambda: deal_out(count - 1, 1).start())
+    for t in range(count - 2, count):
+        hand_on(t)
 
     def got_mine(t):
         pl.when(keeper)(lambda: deal_keep(t).wait())
         pl.when(jnp.logical_not(keeper | across_x))(lambda: deal_on(t).wait_recv())
 
-    for q in range(4):
+    for q in sequence:
         near_copy(x, q).wait_recv()
         part = total[q, here, :] + near[x, q]
         first = (q % 2) * per
@@ -643,9 +673,14 @@
 
         pl.when(across_x)(lambda: deal_on(t).wait_send())
         send(t, e, side_sem, to_y).wait_send()
+        bent = t % 2 == 1 and t < count - 1
+        if bent:
+            pl.when(z < last)(lambda: send(t, first_far, up_sem, to_up).wait_send())
+            pl.when(z > 0)(lambda: send(t, last_far, down_sem, to_down).wait_send())
         for line in range(lines):
             s = 2 * line + y
-            pl.when(line != z)(lambda: send(t, s, side_sem, to_y).wait_send())
+            if not bent or 0 < line < last:
+                pl.when(line != z)(lambda: send(t, s, side_sem, to_y).wait_send())
             pl.when((z < last) & (z >= line))(lambda: send(t, s, up_sem, to_up).wait_send())
             pl.when((z > 0) & (z <= line))(lambda: send(t, s, down_sem, to_down).wait_send())
     for q in range(4):

time: 115 us -> 112 us (0.974)
  Pallas kernels: 113 us -> 110 us
    pallas_call x1, Pallas kernels: 113 us -> 110 us  [fused(): pl.pallas_call(functools.partial(whole_kernel, ex_n, features, tile, earl...]
where the time goes in v3:
time: 112 us
  Pallas kernels  110 us (98%)
  local copies, waits for them, and re-layouts  1.38 us (1%)
    pallas_call x1, Pallas kernels, fused(): pl.pallas_call(functools.partial(whole_kernel, ex_n, features, tile, earl...  110 us

profile of v3, /device:TPU:0, one launch (start us, length us, event | category | flops | bytes accessed | tf_op | source)
XLA Modules:
  0.0 111.6 jit_solution(16394655815038092296)
XLA Ops:
  0.0 110.2 %shard_map.37 = f32[64,128]{1,0:T(8,128)} custom-call(s32[4]{0:T(128)} %words_ref.1, bf16[64,4096]{1,0:T(8,128)(2,1)} %grads_ref.1, bf16[4096,2048]{1,0:T(8,128)(2,1)} %gram_ref.1), custom_call_target="tpu_custom_call" | custom-call | tf_op jit(solution)/shard_map/pallas_call | solution.py:705
  110.2 1.4 %copy.5 = f32[128,64]{0,1:T(8,128)} copy(f32[128,64]{0,1:T(8,128)} %bitcast.1) | data formatting | bytes 65536

commit v4 on v3

--- a/solution.py
+++ b/solution.py
@@ -333,7 +333,10 @@
         pl.semaphore_signal(barrier, inc=1, device_id={"ex": peer}, device_id_type=MESH)
     for peer in others(p, 4):
         pl.semaphore_signal(barrier, inc=1, device_id={"par": peer}, device_id_type=MESH)
-    pl.semaphore_wait(barrier, ex_n + 2)
+    e_far = lax.rem(e + 4, ex_n)
+    to_far = {"ex": e_far, "par": lax.rem(p + 2, 4)}
+    pl.semaphore_signal(barrier, inc=1, device_id=to_far, device_id_type=MESH)
+    pl.semaphore_wait(barrier, ex_n + 3)
 
     to_y, to_z = {"ex": e + 1 - 2 * y}, {"ex": e + 2 - 4 * (z % 2)}
     to_core, to_x = {"par": x * 2 + 1 - c}, {"par": (1 - x) * 2 + c}
@@ -384,11 +387,13 @@
         for part in (0, 1):
             arrived(md, part, g_recv, c)
             gcopy(g2.at[c, md, part], md, part, gc_send, 6 + part, gp_recv, to_core)
+        for keep in keeps:
+            keep.wait()
+
+    def partner_halves():
         for slot in range(4):
             for part in (0, 1):
                 arrived(slot, part, gp_recv, 1 - c)
-        for keep in keeps:
-            keep.wait()
 
     m0 = words_ref[0] | 1
     m2 = words_ref[2] | 1
@@ -495,7 +500,19 @@
         for hop in range(1, lines):
             detour(t - hop - 2, hop)
 
-    @pl.loop(0, early)
+    acc[...] = jnp.zeros_like(acc)
+    for turn in (0, 1):
+        core = c if turn == 0 else 1 - c
+
+        @pl.loop(0, steps)
+        def _(k):
+            add_in(signs[0, core * steps + k], core, k)
+
+        if turn == 0:
+            partner_halves()
+    produced(0)
+
+    @pl.loop(1, early)
     def _(t):
         acc[...] = jnp.zeros_like(acc)
 
@@ -534,6 +551,20 @@
     def deal_out(t, k):
         return rider(deal(t), mine.at[t], fe_send.at[t, k], fe_recv.at[t], (to_core, to_x)[k])
 
+    far_keeper = p == e_far // (ex_n // 4)
+
+    def far_deal(t):
+        return rider(deal(t), mine.at[t], fe_send.at[t, 1], fe_recv.at[t], to_far)
+
+    def goes_far(t):
+        return t >= count // 2 and t % 2 == 1
+
+    def deal_over(t, act):
+        if goes_far(t):
+            pl.when(far_keeper)(lambda: act(far_deal(t)))
+        else:
+            pl.when(keeper)(lambda: act(deal_out(t, 1)))
+
     def deal_on(t):
         return rider(mine.at[t], mine.at[t], fe_send.at[t, 0], fe_recv.at[t], to_core)
 
@@ -543,6 +574,25 @@
             deal_on(t).wait_recv()
             deal_on(t).start()
 
+    rows_of = everyone // 4
+    here = pl.ds(pl.multiple_of(p * rows_of, rows_of), rows_of)
+
+    def rows(qx, qc):
+        return pl.ds(pl.multiple_of((qx * 2 + qc) * rows_of, rows_of), rows_of)
+
+    def near_copy(qx, q):
+        return rider(
+            total.at[q, rows(qx, 1 - c)], near.at[qx, q],
+            cc_send.at[qx, q], cc_recv.at[qx, q], to_core,
+        )
+
+    def far_copy(q):
+        return rider(staged.at[q], far.at[q], cx_send.at[q], cx_recv.at[q], to_x)
+
+    def mark_copy(q):
+        return rider(marks.at[q], far_marks.at[q], cm_send.at[q], cm_recv.at[q], to_x)
+
+    sequence = (0, 2, 1, 3)
     def multiply(t):
         bent = t % 2 == 1 and t < count - 1
         if bent:
@@ -555,14 +605,14 @@
         def _():
             deal_keep(t).start()
             deal_out(t, 0).start()
-            if t < count - 1:
-                deal_out(t, 1).start()
-
-        if t >= 2:
-            hand_on(t - 2)
+
+        if t < count - 1:
+            deal_over(t, lambda copy: copy.start())
+
+        if t >= 4:
+            hand_on(t - 4)
         lhs = jnp.concatenate([feats[t, k].reshape(everyone, tile) for k in range(4)], axis=1)
-        for q in range(4):
-            cols = pl.ds(q * width, width)
+        for q in sequence:
             rhs = jnp.concatenate(
                 [gram[k * piece + t * tile:k * piece + (t + 1) * tile, q * width:(q + 1) * width] for k in range(4)], axis=0
             )
@@ -571,6 +621,8 @@
                 total[q] = part
             else:
                 total[q] += part
+            if t == count - 1:
+                near_copy(1 - x, q).start()
 
     finish(count - 1)
     ready = 0
@@ -586,28 +638,8 @@
     for t in range(ready, count):
         multiply(t)
 
-    rows_of = everyone // 4
-    here = pl.ds(pl.multiple_of(p * rows_of, rows_of), rows_of)
-
-    def rows(qx, qc):
-        return pl.ds(pl.multiple_of((qx * 2 + qc) * rows_of, rows_of), rows_of)
-
-    def near_copy(qx, q):
-        return rider(
-            total.at[q, rows(qx, 1 - c)], near.at[qx, q],
-            cc_send.at[qx, q], cc_recv.at[qx, q], to_core,
-        )
-
-    def far_copy(q):
-        return rider(staged.at[q], far.at[q], cx_send.at[q], cx_recv.at[q], to_x)
-
-    def mark_copy(q):
-        return rider(marks.at[q], far_marks.at[q], cm_send.at[q], cm_recv.at[q], to_x)
-
-    sequence = (0, 2, 1, 3)
-    for qx in (1 - x, x):
-        for q in sequence:
-            near_copy(qx, q).start()
+    for q in sequence:
+        near_copy(x, q).start()
     for q in sequence:
         near_copy(1 - x, q).wait_recv()
         part = total[q, rows(1 - x, c), :] + near[1 - x, q]
@@ -618,8 +650,8 @@
         mark_copy(q).start()
         far_copy(q).start()
         if q == sequence[2]:
-            pl.when(keeper)(lambda: deal_out(count - 1, 1).start())
-    for t in range(count - 2, count):
+            deal_over(count - 1, lambda copy: copy.start())
+    for t in range(count - 4, count):
         hand_on(t)
 
     def got_mine(t):
@@ -666,10 +698,8 @@
     for t in range(count):
         x_copy(t).wait_send()
 
-        @pl.when(keeper)
-        def _():
-            deal_out(t, 1).wait_send()
-            deal_out(t, 0).wait_send()
+        deal_over(t, lambda copy: copy.wait_send())
+        pl.when(keeper)(lambda: deal_out(t, 0).wait_send())
 
         pl.when(across_x)(lambda: deal_on(t).wait_send())
         send(t, e, side_sem, to_y).wait_send()

time: 112 us -> 110 us (0.982)
  Pallas kernels: 110 us -> 108 us
    pallas_call x1, Pallas kernels: 110 us -> 108 us  [fused(): pl.pallas_call(functools.partial(whole_kernel, ex_n, features, tile, earl...]
where the time goes in v4:
time: 110 us; the launch traced here: 109 us
  Pallas kernels  108 us (98%)
  local copies, waits for them, and re-layouts  1.38 us (1%)
    pallas_call x1, Pallas kernels, fused(): pl.pallas_call(functools.partial(whole_kernel, ex_n, features, tile, earl...  108 us

profile of v4, /device:TPU:0, one launch (start us, length us, event | category | flops | bytes accessed | tf_op | source)
XLA Modules:
  0.0 109.3 jit_solution(5052161683088614170)
XLA Ops:
  0.0 107.9 %shard_map.37 = f32[64,128]{1,0:T(8,128)} custom-call(s32[4]{0:T(128)} %words_ref.1, bf16[64,4096]{1,0:T(8,128)(2,1)} %grads_ref.1, bf16[4096,2048]{1,0:T(8,128)(2,1)} %gram_ref.1), custom_call_target="tpu_custom_call" | custom-call | tf_op jit(solution)/shard_map/pallas_call | solution.py:735
  107.9 1.4 %copy.5 = f32[128,64]{0,1:T(8,128)} copy(f32[128,64]{0,1:T(8,128)} %bitcast.1) | data formatting | bytes 65536
